TPU v7x, 512 devices: a whole 4x4x16 slice. The times are simulated.
512 devices in a mesh: dp: 16 (over z_hi, x), row: 8 (over y, core), col: 4 (over z_lo).
Axes of the slice: x: 4, y: 4, z: 16 (z_hi: 4, z_lo: 4; z = z_hi * 4 + z_lo), core: 2. Of those that a mesh axis runs over, the one named last changes fastest.
Arguments:
- tokens: bfloat16 [4096, 4096], P('dp', 'col'), may hold values from -6 to 6
- cotangent: bfloat16 [4096, 4096], P('dp', 'col'), may hold values from -6 to 6
- counts: int32 [16], P('dp'), may hold values from 1 to 4, as said below
- up_blocks: bfloat16 [4, 8, 32, 128, 128], P('col', 'row'), may hold values from -0.1875 to 0.1875
- up_rows: int32 [4, 8, 32], P('col', 'row'), may hold values from 0 to 7, as said below
- up_cols: int32 [4, 8, 32], P('col', 'row'), may hold values from 0 to 15, as said below
- down_blocks: bfloat16 [8, 4, 32, 128, 128], P('row', 'col'), may hold values from -0.09375 to 0.09375
- down_rows: int32 [8, 4, 32], P('row', 'col'), may hold values from 0 to 15, as said below
- down_cols: int32 [8, 4, 32], P('row', 'col'), may hold values from 0 to 7, as said below
Outputs:
- y_out: bfloat16 [4096, 4096], P('dp', 'col')
- grad_tokens: bfloat16 [4096, 4096], P('dp', 'col')
- grad_up: float32 [4, 8, 32, 128, 128], P('col', 'row', 'dp')
- grad_down: float32 [8, 4, 32, 128, 128], P('row', 'col', 'dp')
Inputs may be any that keep to these rules, and one draw needn't show every extreme that they name: Replica d has counts[d] live microbatches of 64 tokens in its first slots; the rest of its 4 slots are padding. `up_rows`: within each tile the 32 blocks stand at distinct positions, and every tile holds its block (0, 0) and its block (7, 15). `up_cols`: paired with up_rows as above. `down_rows`: within each tile the 32 blocks stand at distinct positions, and every tile holds its block (0, 0) and its block (15, 7). `down_cols`: paired with down_rows as above.
All inputs are finite; a program needn't handle non-finite values.
Results may differ from a plain program's by a relative error of at most 0.029.
Values may be sent and summed in bfloat16 or wider, within the bound.
A program may use at most 64 MiB of HBM per device.

v0:
```python
import jax
import jax.numpy as jnp
from jax import lax
from jax.sharding import PartitionSpec as P

FF = 16384
MB_TOK = 64


def gelu_exact(hidden_in):
    return 0.5 * hidden_in * (1.0 + jax.scipy.special.erf(hidden_in * 0.7071067811865476))


def gelu_slope(hidden_in):
    normal_cdf = 0.5 * (1.0 + jax.scipy.special.erf(hidden_in * 0.7071067811865476))
    return normal_cdf + hidden_in * jnp.exp(-0.5 * hidden_in * hidden_in) * 0.3989422804014327


def sparse_apply(operand, blocks, in_index, out_index, out_count, flipped):
    row_count = operand.shape[0]
    block_size = blocks.shape[-1]
    selected = jnp.take(operand.reshape(row_count, -1, block_size), in_index, axis=1)
    pattern = "tnj,nkj->tnk" if flipped else "tnk,nkj->tnj"
    products = jnp.einsum(pattern, selected, blocks, preferred_element_type=jnp.float32)
    placing = (out_index[:, None] == jnp.arange(out_count, dtype=jnp.int32)[None, :]).astype(
        jnp.bfloat16
    )
    upper_part = products.astype(jnp.bfloat16)
    lower_part = (products - upper_part.astype(jnp.float32)).astype(jnp.bfloat16)
    combined = jnp.einsum("tnj,nb->tbj", upper_part, placing, preferred_element_type=jnp.float32)
    combined = combined + jnp.einsum(
        "tnj,nb->tbj", lower_part, placing, preferred_element_type=jnp.float32
    )
    return combined.reshape(row_count, out_count * block_size)


def slab_terms(left_side, right_side, left_index, right_index, block_size):
    row_count = left_side.shape[0]
    left_slab = jnp.take(left_side.reshape(row_count, -1, block_size), left_index, axis=1)
    right_slab = jnp.take(right_side.reshape(row_count, -1, block_size), right_index, axis=1)
    return jnp.einsum("tnk,tnj->nkj", left_slab, right_slab, preferred_element_type=jnp.float32)


def body(tokens, cotangent, counts, up_blocks, up_rows, up_cols, down_blocks, down_rows, down_cols):
    capacity = tokens.shape[0]
    block_size = up_blocks.shape[-1]
    tile_width = tokens.shape[1] // block_size
    tile_hidden = FF // lax.axis_size("row") // block_size
    up_tile = up_blocks[0, 0]
    up_from = up_rows[0, 0]
    up_into = up_cols[0, 0]
    down_tile = down_blocks[0, 0]
    down_from = down_rows[0, 0]
    down_into = down_cols[0, 0]
    total_count = lax.psum(counts[0], "dp").astype(jnp.float32)
    live_rows = (jnp.arange(capacity, dtype=jnp.int32) // MB_TOK < counts[0]).astype(jnp.float32)[
        :, None
    ]
    partial_hidden = sparse_apply(tokens, up_tile, up_from, up_into, tile_hidden, False)
    hidden = lax.psum(partial_hidden.astype(jnp.bfloat16), "col").astype(jnp.float32)
    activation = gelu_exact(hidden).astype(jnp.bfloat16)
    partial_output = sparse_apply(activation, down_tile, down_from, down_into, tile_width, False)
    output_sum = lax.psum(partial_output.astype(jnp.bfloat16), "row").astype(jnp.float32)
    y_out = (output_sum * live_rows).astype(jnp.bfloat16)
    grad_mask = cotangent * live_rows.astype(jnp.bfloat16)
    partial_act = sparse_apply(grad_mask, down_tile, down_into, down_from, tile_hidden, True)
    act_grad = lax.psum(partial_act.astype(jnp.bfloat16), "col").astype(jnp.float32)
    hidden_grad = (act_grad * gelu_slope(hidden)).astype(jnp.bfloat16)
    partial_input = sparse_apply(hidden_grad, up_tile, up_into, up_from, tile_width, True)
    grad_tokens = lax.psum(partial_input.astype(jnp.bfloat16), "row")
    up_share, down_share = (
        lax.psum_scatter(
            slab_terms(tokens, hidden_grad, up_from, up_into, block_size).astype(jnp.bfloat16),
            "dp",
            scatter_dimension=0,
            tiled=True,
        ).astype(jnp.float32),
        lax.psum_scatter(
            slab_terms(activation, grad_mask, down_from, down_into, block_size).astype(
                jnp.bfloat16
            ),
            "dp",
            scatter_dimension=0,
            tiled=True,
        ).astype(jnp.float32),
    )
    grad_up = (up_share / total_count)[None, None]
    grad_down = (down_share / total_count)[None, None]
    return (y_out, grad_tokens, grad_up, grad_down)


def solution(mesh):
    return jax.shard_map(
        body,
        mesh=mesh,
        in_specs=(
            P("dp", "col"),
            P("dp", "col"),
            P("dp"),
            P("col", "row", None, None, None),
            P("col", "row", None),
            P("col", "row", None),
            P("row", "col", None, None, None),
            P("row", "col", None),
            P("row", "col", None),
        ),
        out_specs=(
            P("dp", "col"),
            P("dp", "col"),
            P("col", "row", "dp", None, None),
            P("row", "col", "dp", None, None),
        ),
        check_vma=False,
    )
```

profile of v0, /device:TPU:1, one launch (start us, length us, event | category | flops | bytes accessed | tf_op | source)
XLA Modules:
  0.0 481.7 jit_solution(6578266980955588375)
XLA Ops:
  7.2 0.0 all-reduce.7.cloned.1.call-start
  7.2 0.8 compare_and_fusion.3
  8.0 0.7 compare_select_fusion.3
  8.7 0.7 compare_and_fusion.1
  9.3 0.7 compare_select_fusion.1
  10.7 1.2 copy.33
  11.9 0.3 copy.34
  12.2 0.2 copy.41
  12.5 0.3 copy.42
  12.8 2.2 gather_fusion
  14.9 2.4 fusion.3
  17.3 1.3 fusion.39
  18.6 1.4 fusion.57
  20.0 1.6 copy.53
  21.5 2.1 gather_fusion.2
  23.7 2.4 fusion.1
  26.1 1.3 fusion.31
  27.3 1.4 fusion.60
  28.7 1.6 copy.54
  30.3 0.0 all-reduce.7.cloned.1.call-update
  30.4 0.2 all-reduce.5.cloned.1.call-start
  30.7 113.6 %all-reduce.7.cloned.1.call-done = (bf16[256,2048]{0,1:T(8,128)(2,1)}, bf16[256,2048]{0,1:T(8,128)(2,1)}) async-done(((bf16[256,2048]{0,1:T(8,128)(2,1)}, bf16[256,2048]{0,1:T(8,128)(2,1)}), (bf16[256,2048]{0,1:T(8,128)(2,1)}, bf16[256,2048]{0,1:T(8,128)(2,1)})) %all-reduce.7.cloned.1.call-update) | async-done | bytes 2097168 | tf_op jit(solution)/shard_map/psum | solution.py:60
  144.3 3.2 fusion.12
  147.5 0.7 copy.46
  148.1 1.6 copy.38
  149.8 2.2 gather_fusion.1
  151.9 2.2 gather_fusion.3
  154.1 2.4 fusion
  156.5 1.2 fusion.27
  157.7 1.3 fusion.69
  159.0 0.3 copy-done.2
  159.3 0.3 copy-done.4
  159.6 0.8 fusion.2
  160.4 1.2 fusion.35
  161.6 1.3 fusion.72
  162.9 1.2 copy_bitcast_fusion
  164.1 0.0 reduce-scatter.5.cloned.1.call-start
  164.2 4.4 fusion.47
  168.6 0.0 reduce-scatter.3.cloned.1.call-start
  168.6 3.5 fusion.52
  172.2 19.1 %psum.39 = s32[]{:T(128)} all-reduce(s32[]{:T(128)} %bitcast.17), channel_id=1, replica_groups=mesh['dp'=16,'row'=8,'col'=4] {'dp'}, use_global_device_ids=true, to_apply=%region_5.8 | all-reduce | flops 1 | bytes 8 | tf_op jit(solution)/shard_map/psum | solution.py:55
  191.9 48.7 %all-reduce.5.cloned.1.call-done = (bf16[256,1024]{1,0:T(8,128)(2,1)}, bf16[256,1024]{1,0:T(8,128)(2,1)}) async-done(((bf16[256,1024]{1,0:T(8,128)(2,1)}, bf16[256,1024]{1,0:T(8,128)(2,1)}), (bf16[256,1024]{1,0:T(8,128)(2,1)}, bf16[256,1024]{1,0:T(8,128)(2,1)})) %all-reduce.5.cloned.1.call-update) | async-done | bytes 1048592 | tf_op jit(solution)/shard_map/psum | solution.py:63
  240.7 2.0 multiply_convert_fusion
  242.7 117.0 %reduce-scatter.5.cloned.1.call-done = bf16[2,128,128]{2,1,0:T(8,128)(2,1)} async-done(((bf16[32,128,128]{2,1,0:T(8,128)(2,1)}), bf16[2,128,128]{2,1,0:T(8,128)(2,1)}) %reduce-scatter.5.cloned.1.call-update) | async-done | bytes 65552 | tf_op jit(solution)/shard_map/reduce_scatter | solution.py:78
  359.6 1.5 divide_bitcast_fusion
  361.1 110.7 %reduce-scatter.3.cloned.1.call-done = bf16[2,128,128]{2,1,0:T(8,128)(2,1)} async-done(((bf16[32,128,128]{2,1,0:T(8,128)(2,1)}), bf16[2,128,128]{2,1,0:T(8,128)(2,1)}) %reduce-scatter.3.cloned.1.call-update) | async-done | bytes 65552 | tf_op jit(solution)/shard_map/reduce_scatter | solution.py:72
  471.8 1.5 divide_bitcast_fusion.1
  473.3 1.9 copy.96
  (32 shorter events, 0.2 us)
Async XLA Ops:
  7.2 7.8 %copy-start = (bf16[1,1,32,128,128]{4,3,2,1,0:T(8,128)(2,1)S(1)}, bf16[1,1,32,128,128]{4,3,2,1,0:T(8,128)(2,1)}, u32[]{:S(2)}) copy-start(bf16[1,1,32,128,128]{4,3,2,1,0:T(8,128)(2,1)} %param.16) | copy-start | bytes 3145732
  7.2 5.0 %copy-start.5 = (bf16[256,1024]{1,0:T(8,128)(2,1)S(1)}, bf16[256,1024]{1,0:T(8,128)(2,1)}, u32[]{:S(2)}) copy-start(bf16[256,1024]{1,0:T(8,128)(2,1)} %param.14) | copy-start | bytes 1572868
  7.2 137.1 %all-reduce.7.cloned.1.call-start = ((), (), s32[]{:S(2)}) async-start(), calls=%async_computation.5 | async-start | bytes 4194304 | tf_op jit(solution)/shard_map/psum | solution.py:60
  14.9 2.4 copy-start.6
  21.5 2.1 copy-start.3
  23.7 2.4 copy-start.7
  30.4 210.3 %all-reduce.5.cloned.1.call-start = ((), (), s32[]{:S(2)}) async-start(), calls=%async_computation.4 | async-start | bytes 2097152 | tf_op jit(solution)/shard_map/psum | solution.py:63
  154.1 2.4 copy-start.8
  157.7 1.6 copy-start.2
  157.7 1.9 copy-start.4
  159.6 0.8 copy-start.9
  164.1 4.5 copy-start.1
  164.1 195.5 %reduce-scatter.5.cloned.1.call-start = ((), (), s32[]{:S(2)}) async-start(), calls=%async_computation.3 | async-start | bytes 1114112 | tf_op jit(solution)/shard_map/reduce_scatter | solution.py:78
  168.6 303.3 %reduce-scatter.3.cloned.1.call-start = ((), (), s32[]{:S(2)}) async-start(), calls=%async_computation.2 | async-start | bytes 1114112 | tf_op jit(solution)/shard_map/reduce_scatter | solution.py:72
Sparse Core Ops, SparseCore 0:
  30.5 113.7 all-reduce.6
  164.2 76.3 all-reduce.4
  245.3 114.2 reduce-scatter.4
  363.6 108.2 reduce-scatter.2
where the time goes:
time: 482 us
  waiting for transfers between devices  390 us (81%)
  matrix products  26.2 us (5%)
  local copies, waits for them, and re-layouts  19.7 us (4%)
  blocking collectives  19.1 us (4%)
  between operations  15.3 us (3%)
  other arithmetic  11 us (2%)
    reduce_scatter x1, waiting for transfers between devices, body(): lax.psum_scatter(slab_terms(activation, grad_mask, down_from, down_into,...  117 us
    psum x1, waiting for transfers between devices, body(): lax.psum(partial_hidden.astype(jnp.bfloat16), 'col').astype(jnp.float32)  114 us
    reduce_scatter x1, waiting for transfers between devices, body(): lax.psum_scatter(slab_terms(tokens, hidden_grad, up_from, up_into, block_...  111 us
    psum x1, waiting for transfers between devices, body(): lax.psum(partial_output.astype(jnp.bfloat16), 'row').astype(jnp.float32)  48.7 us
    psum x1, blocking collectives, body(): total_count = lax.psum(counts[0], 'dp').astype(jnp.float32)  19.1 us
  transfers between devices with their start and end apart: 4, of which 4 were waited for; matrix products, arithmetic and copies ran while one was open for 2% of the time, Pallas kernels for 0%

commit v1 on v0

v1 whole, which is shorter than its diff:
```python
import jax
import jax.numpy as jnp
from jax import lax
from jax.experimental import pallas as pl
from jax.experimental.pallas import tpu as pltpu
from jax.sharding import PartitionSpec as P

MESH = pl.DeviceIdType.MESH
BF = jnp.bfloat16
F32 = jnp.float32
B = 128
CAP = 256
MB_TOK = 64
STEPS = 8
TD = 8
NB = 32
LAG = 4
CH = 2 * B + 16
QR = 32

NT = (((1,), (1,)), ((), ()))
NN = (((1,), (0,)), ((), ()))


def dot(a, b, dims=NN):
    return lax.dot_general(a, b, dims, preferred_element_type=F32)


def kernel(
    counts, inv_up, inv_down, up_rows, up_cols, down_rows, down_cols,
    tokens, cotangent, up_blocks, down_blocks,
    y_out, g_out, gu_out, gd_out,
    gm, tok_t, gm_t, wup, wdn, part, rbuf, ah, yacc, gacc,
    fs, fr, ys, yr, yo, gbuf, xr, zbuf, zr,
    rs_s, rs_r, ag_s, ag_r, f_s, f_r, y_s, y_r, ya_s, ya_r, sb_s, sb_r, x_s, x_r, z_s, z_r,
):
    c = lax.axis_index("col")
    row = lax.axis_index("row")
    dp = lax.axis_index("dp")
    core = row % 2
    yi = row // 2
    hi = dp // 4
    xi = dp % 4
    count = counts[0]

    sibling = {"row": row + 1 - 2 * core}
    y_right = {"row": (row + 2) % 8}
    y_left = {"row": (row + 6) % 8}
    x_right = {"dp": hi * 4 + (xi + 1) % 4}
    x_left = {"dp": hi * 4 + (xi + 3) % 4}
    z_right = {"dp": ((hi + 1) % 4) * 4 + xi}
    z_left = {"dp": ((hi + 3) % 4) * 4 + xi}

    def send(src, dst, s_sem, r_sem, device):
        return pltpu.make_async_remote_copy(
            src_ref=src, dst_ref=dst, send_sem=s_sem, recv_sem=r_sem,
            device_id=device, device_id_type=MESH,
        )

    barrier = pltpu.get_barrier_semaphore()
    for peer in (sibling, y_right, y_left, x_right, x_left, z_right, z_left):
        pl.semaphore_signal(barrier, inc=1, device_id=peer, device_id_type=MESH)

    @pl.when(c > 0)
    def _():
        pl.semaphore_signal(barrier, inc=1, device_id={"col": c - 1}, device_id_type=MESH)

    @pl.when(c < 3)
    def _():
        pl.semaphore_signal(barrier, inc=1, device_id={"col": c + 1}, device_id_type=MESH)

    live = (lax.broadcasted_iota(jnp.int32, (CAP, 1), 0) // MB_TOK < count).astype(F32)
    gm[...] = (cotangent[...].astype(F32) * live).astype(BF)

    inside = jnp.where((c > 0) & (c < 3), 1, 0)
    pl.semaphore_wait(barrier, 8 + inside)

    def place(s):
        q = c + s * (3 - 2 * c)
        return q, c + 1 - 2 * s, c - 1 + 2 * s

    def rs_copy(j, device):
        return send(rbuf.at[j], rbuf.at[j], rs_s.at[j], rs_r.at[j], {"col": device})

    def ag_copy(j, device):
        return send(ah.at[j], ah.at[j], ag_s.at[j], ag_r.at[j], {"col": device})

    def partials(k, carry):
        for s in range(2):
            for i in range(TD):
                iu = inv_up[i * 16 + k + 8 * s]
                blk = up_blocks[jnp.minimum(iu, NB - 1)]
                wup[k, i * B:(i + 1) * B, s * B:(s + 1) * B] = jnp.where(iu < NB, blk, jnp.zeros_like(blk))
                idn = inv_down[(k + 8 * s) * 8 + i]
                blk = down_blocks[jnp.minimum(idn, NB - 1)]
                wdn[k, s * B:(s + 1) * B, i * B:(i + 1) * B] = jnp.where(idn < NB, blk, jnp.zeros_like(blk))
        hp = dot(tokens[...], wup[k])
        ap = dot(gm[...], wdn[k], NT)
        for s in range(2):
            part[k + 8 * s, 0] = hp[:, s * B:(s + 1) * B]
            part[k + 8 * s, 1] = ap[:, s * B:(s + 1) * B]

        @pl.when(c == 0)
        def _():
            rbuf[k, 0] = hp[:, :B].astype(BF)
            rbuf[k, 1] = ap[:, :B].astype(BF)
            rs_copy(k, 1).start()

        @pl.when(c == 3)
        def _():
            rbuf[k + 8, 0] = hp[:, B:].astype(BF)
            rbuf[k + 8, 1] = ap[:, B:].astype(BF)
            rs_copy(k + 8, 2).start()

        return carry

    lax.fori_loop(0, STEPS, partials, 0)

    yacc[...] = jnp.zeros_like(yacc)
    gacc[...] = jnp.zeros_like(gacc)
    for i in range(TD):
        tok_t[i] = tokens[:, i * B:(i + 1) * B].T
        gm_t[i] = gm[:, i * B:(i + 1) * B].T

    first = c // 2

    def sum_step(k, s):
        q, nxt, prv = place(s)
        j = s * 8 + k

        @pl.when(q > 0)
        def _():
            rs_copy(j, nxt).wait_recv()

        @pl.when((q > 0) & (q < 3))
        def _():
            rbuf[j] = (rbuf[j].astype(F32) + part[j]).astype(BF)
            rs_copy(j, nxt).start()

        @pl.when(q == 3)
        def _():
            h = rbuf[j, 0].astype(F32) + part[j, 0]
            a = rbuf[j, 1].astype(F32) + part[j, 1]
            cdf = 0.5 * (1.0 + lax.erf(h * 0.7071067811865476))
            ah[j, 0] = (h * cdf).astype(BF)
            slope = cdf + h * jnp.exp(-0.5 * h * h) * 0.3989422804014327
            ah[j, 1] = (a * slope).astype(BF)
            ag_copy(j, prv).start()

    def share_step(k, s):
        q, nxt, prv = place(s)
        j = s * 8 + k

        @pl.when(q < 3)
        def _():
            ag_copy(j, prv).wait_recv()

        @pl.when((q > 0) & (q < 3))
        def _():
            ag_copy(j, prv).start()

    def use_step(k):
        act = jnp.concatenate([ah[k, 0], ah[k + 8, 0]], axis=1)
        yacc[...] += dot(act, wdn[k])
        hg = jnp.concatenate([ah[k, 1], ah[k + 8, 1]], axis=1)
        gacc[...] += dot(hg, wup[k], NT)

    def line(it, carry):
        @pl.when(it < STEPS)
        def _():
            sum_step(it, first)
            sum_step(it, 1 - first)

        @pl.when(it >= LAG)
        def _():
            share_step(it - LAG, 1 - first)
            share_step(it - LAG, first)
            use_step(it - LAG)

        return carry

    lax.fori_loop(0, STEPS + LAG, line, 0)

    mine = pl.multiple_of(core * B, B)
    other = pl.multiple_of((1 - core) * B, B)
    fs[0] = yacc[pl.ds(other, B), :].astype(BF)
    fs[1] = gacc[pl.ds(other, B), :].astype(BF)
    pair = send(fs, fr, f_s, f_r, sibling)
    pair.start()

    count_rows = jnp.zeros((16, B), F32) + count.astype(F32)

    def grads(t, zh):
        def body(xq, carry):
            for b in range(2):
                k = (zh * 4 + xq) * 2 + b
                gu = dot(tok_t[up_rows[k]], ah[up_cols[k], 1])
                gbuf[0, t, xq, b * B:(b + 1) * B, :] = gu.astype(BF)
                gd = dot(gm_t[down_cols[k]], ah[down_rows[k], 0])
                gbuf[1, t, xq, b * B:(b + 1) * B, :] = gd.astype(BF)
            gbuf[0, t, xq, 2 * B:, :] = count_rows.astype(BF)
            gbuf[1, t, xq, 2 * B:, :] = count_rows.astype(BF)
            return carry

        lax.fori_loop(0, 4, body, 0)

    order = [(hi + 2) % 4, (hi + 1) % 4, (hi + 3) % 4, hi]
    x1, x2, x3 = (xi + 1) % 4, (xi + 2) % 4, (xi + 3) % 4

    def x_msg(t, m):
        src = (
            gbuf.at[0, t, x2], gbuf.at[1, t, x2], gbuf.at[1, t, x1], gbuf.at[0, t, x3],
            xr.at[t, 0], xr.at[t, 1],
        )[m]
        return send(src, xr.at[t, m], x_s.at[t, m], x_r.at[t, m], x_left if m % 2 else x_right)

    def x_start(t):
        for m in range(4):
            x_msg(t, m).start()

    def x_relay(t):
        x_msg(t, 0).wait_recv()
        xr[t, 0] = (xr[t, 0].astype(F32) + gbuf[0, t, x1].astype(F32)).astype(BF)
        x_msg(t, 4).start()
        x_msg(t, 1).wait_recv()
        xr[t, 1] = (xr[t, 1].astype(F32) + gbuf[1, t, x3].astype(F32)).astype(BF)
        x_msg(t, 5).start()

    def x_final(t):
        for m in range(2, 6):
            x_msg(t, m).wait_recv()
        zbuf[0, t] = (gbuf[0, t, xi].astype(F32) + xr[t, 3].astype(F32) + xr[t, 4].astype(F32)).astype(BF)
        zbuf[1, t] = (gbuf[1, t, xi].astype(F32) + xr[t, 2].astype(F32) + xr[t, 5].astype(F32)).astype(BF)

    def z_msg(m):
        src = (zbuf.at[0, 0], zbuf.at[1, 0], zbuf.at[1, 1], zbuf.at[0, 2], zr.at[0], zr.at[1])[m]
        return send(src, zr.at[m], z_s.at[m], z_r.at[m], z_left if m % 2 else z_right)

    def y_msg(m):
        src = (ys.at[0], ys.at[1], ys.at[2], ys.at[3], yr.at[0], yr.at[1])[m]
        return send(src, yr.at[m], y_s.at[m], y_r.at[m], y_left if m % 2 else y_right)

    def rows_of(acc, chunk):
        return acc[pl.ds(pl.multiple_of(core * B + chunk * QR, QR), QR), :]

    y1, y2, y3 = (yi + 1) % 4, (yi + 2) % 4, (yi + 3) % 4

    def y_share(m):
        g0 = core * 4 + yi
        if m < 2:
            ref = yo.at[g0]
        elif m == 2:
            ref = yo.at[core * 4 + y3, 0]
        else:
            ref = yo.at[core * 4 + y1, 1]
        return send(ref, ref, ya_s.at[m], ya_r.at[m], y_left if m % 2 else y_right)

    def y_arrived(m):
        if m == 0:
            ref = yo.at[core * 4 + y3]
        elif m == 1:
            ref = yo.at[core * 4 + y1]
        else:
            ref = yo.at[core * 4 + y2, m - 2]
        return send(ref, ref, ya_s.at[m], ya_r.at[m], y_left if m % 2 else y_right)

    def twin(m, half):
        ref = yo.at[half * 4 + (yi, y3, y1, y2)[m]]
        return send(ref, ref, sb_s.at[m], sb_r.at[m], sibling)

    grads(0, order[0])
    x_start(0)

    pair.wait_recv()
    yacc[pl.ds(mine, B), :] += fr[0].astype(F32)
    gacc[pl.ds(mine, B), :] += fr[1].astype(F32)
    ys[0] = rows_of(yacc, y2).astype(BF)
    ys[1] = rows_of(gacc, y2).astype(BF)
    ys[2] = rows_of(gacc, y1).astype(BF)
    ys[3] = rows_of(yacc, y3).astype(BF)
    for m in range(4):
        y_msg(m).start()

    grads(1, order[1])
    x_start(1)
    x_relay(0)

    y_msg(0).wait_recv()
    yr[0] = (yr[0].astype(F32) + rows_of(yacc, y1)).astype(BF)
    y_msg(4).start()
    y_msg(1).wait_recv()
    yr[1] = (yr[1].astype(F32) + rows_of(gacc, y3)).astype(BF)
    y_msg(5).start()

    grads(2, order[2])
    x_start(2)
    x_relay(1)
    x_final(0)
    z_msg(0).start()
    z_msg(1).start()

    for m in range(2, 6):
        y_msg(m).wait_recv()
    live_chunk = (core * 2 + yi // 2 < count).astype(F32)
    y_sum = rows_of(yacc, yi) + yr[3].astype(F32) + yr[4].astype(F32)
    yo[core * 4 + yi, 0] = (y_sum * live_chunk).astype(BF)
    yo[core * 4 + yi, 1] = (rows_of(gacc, yi) + yr[2].astype(F32) + yr[5].astype(F32)).astype(BF)
    y_share(0).start()
    y_share(1).start()
    twin(0, core).start()

    grads(3, order[3])
    x_start(3)
    x_relay(2)
    x_final(1)
    z_msg(2).start()

    y_arrived(0).wait_recv()
    y_share(2).start()
    twin(1, core).start()
    y_arrived(1).wait_recv()
    y_share(3).start()
    twin(2, core).start()

    z_msg(0).wait_recv()
    zr[0] = (zr[0].astype(F32) + zbuf[0, 1].astype(F32)).astype(BF)
    z_msg(4).start()

    x_relay(3)
    x_final(2)
    z_msg(3).start()
    z_msg(1).wait_recv()
    zr[1] = (zr[1].astype(F32) + zbuf[1, 2].astype(F32)).astype(BF)
    z_msg(5).start()

    y_arrived(2).wait_recv()
    y_arrived(3).wait_recv()
    twin(3, core).start()

    x_final(3)
    for m in range(4):
        twin(m, 1 - core).wait_recv()
    for half in range(2):
        for chunk in range(4):
            at = half * B + chunk * QR
            y_out[at:at + QR, :] = yo[half * 4 + chunk, 0]
            g_out[at:at + QR, :] = yo[half * 4 + chunk, 1]

    for m in range(2, 6):
        z_msg(m).wait_recv()
    gu_sum = zbuf[0, 3].astype(F32) + zr[3].astype(F32) + zr[4].astype(F32)
    gd_sum = zbuf[1, 3].astype(F32) + zr[2].astype(F32) + zr[5].astype(F32)
    total = gu_sum[2 * B:2 * B + 1, :]
    for b in range(2):
        gu_out[b] = gu_sum[b * B:(b + 1) * B, :] / total
        gd_out[b] = (gd_sum[b * B:(b + 1) * B, :] / total).T

    for s in range(2):
        q, nxt, prv = place(s)

        @pl.when(q < 3)
        def _(s=s, nxt=nxt):
            lax.fori_loop(0, STEPS, lambda k, v: (rs_copy(s * 8 + k, nxt).wait_send(), v)[1], 0)

        @pl.when(q > 0)
        def _(s=s, prv=prv):
            lax.fori_loop(0, STEPS, lambda k, v: (ag_copy(s * 8 + k, prv).wait_send(), v)[1], 0)

    pair.wait_send()
    for m in range(6):
        y_msg(m).wait_send()
        z_msg(m).wait_send()
        for t in range(4):
            x_msg(t, m).wait_send()
    for m in range(4):
        y_share(m).wait_send()
        twin(m, core).wait_send()


def inverse(position):
    slots = jnp.arange(B, dtype=jnp.int32)
    order = jnp.arange(NB, dtype=jnp.int32)
    hit = position[None, :] == slots[:, None]
    return NB - jnp.sum(jnp.where(hit, NB - order[None, :], 0), axis=1).astype(jnp.int32)


def body(tokens, cotangent, counts, up_blocks, up_rows, up_cols, down_blocks, down_rows, down_cols):
    ur, uc = up_rows[0, 0], up_cols[0, 0]
    dr, dc = down_rows[0, 0], down_cols[0, 0]
    inv_up = inverse(ur * 16 + uc)
    inv_down = inverse(dr * 8 + dc)
    smem = pl.BlockSpec(memory_space=pltpu.SMEM)
    vmem = pl.BlockSpec(memory_space=pltpu.VMEM)
    width = TD * B
    dma = pltpu.SemaphoreType.DMA
    y_out, g_out, gu, gd = pl.pallas_call(
        kernel,
        out_shape=(
            jax.ShapeDtypeStruct((CAP, width), BF),
            jax.ShapeDtypeStruct((CAP, width), BF),
            jax.ShapeDtypeStruct((2, B, B), F32),
            jax.ShapeDtypeStruct((2, B, B), F32),
        ),
        in_specs=[smem] * 7 + [vmem] * 4,
        out_specs=(vmem,) * 4,
        scratch_shapes=[
            pltpu.VMEM((CAP, width), BF),
            pltpu.VMEM((TD, B, CAP), BF),
            pltpu.VMEM((TD, B, CAP), BF),
            pltpu.VMEM((STEPS, width, 2 * B), BF),
            pltpu.VMEM((STEPS, 2 * B, width), BF),
            pltpu.VMEM((16, 2, CAP, B), F32),
            pltpu.VMEM((16, 2, CAP, B), BF),
            pltpu.VMEM((16, 2, CAP, B), BF),
            pltpu.VMEM((CAP, width), F32),
            pltpu.VMEM((CAP, width), F32),
            pltpu.VMEM((2, B, width), BF),
            pltpu.VMEM((2, B, width), BF),
            pltpu.VMEM((4, QR, width), BF),
            pltpu.VMEM((6, QR, width), BF),
            pltpu.VMEM((8, 2, QR, width), BF),
            pltpu.VMEM((2, 4, 4, CH, B), BF),
            pltpu.VMEM((4, 6, CH, B), BF),
            pltpu.VMEM((2, 4, CH, B), BF),
            pltpu.VMEM((6, CH, B), BF),
            dma((16,)), dma((16,)), dma((16,)), dma((16,)),
            dma, dma, dma((6,)), dma((6,)), dma((4,)), dma((4,)), dma((4,)), dma((4,)),
            dma((4, 6)), dma((4, 6)), dma((6,)), dma((6,)),
        ],
        compiler_params=pltpu.CompilerParams(
            collective_id=0, has_side_effects=True, vmem_limit_bytes=56 << 20
        ),
    )(counts, inv_up, inv_down, ur, uc, dr, dc, tokens, cotangent, up_blocks[0, 0], down_blocks[0, 0])
    return y_out, g_out, gu[None, None], gd[None, None]


def solution(mesh):
    return jax.shard_map(
        body,
        mesh=mesh,
        in_specs=(
            P("dp", "col"),
            P("dp", "col"),
            P("dp"),
            P("col", "row", None, None, None),
            P("col", "row", None),
            P("col", "row", None),
            P("row", "col", None, None, None),
            P("row", "col", None),
            P("row", "col", None),
        ),
        out_specs=(
            P("dp", "col"),
            P("dp", "col"),
            P("col", "row", "dp", None, None),
            P("row", "col", "dp", None, None),
        ),
        check_vma=False,
    )
```

time: 482 us -> 143 us (0.30)
  waiting for transfers between devices: 390 us -> 0 us
  Pallas kernels: 0 us -> 135 us
  matrix products: 26.2 us -> 0 us
  blocking collectives: 19.1 us -> 0 us
  between operations: 15.3 us -> 1.32 us
  local copies, waits for them, and re-layouts: 19.7 us -> 5.88 us
  other arithmetic: 11 us -> 0.62 us
    reduce_scatter x2 -> x0, waiting for transfers between devices: 228 us -> none  [the longest x1 117 us: body(): lax.psum_scatter(slab_terms(activation, grad_mask, down_from, down_into,...]
    psum x2 -> x0, waiting for transfers between devices: 162 us -> none  [the longest x1 114 us: body(): lax.psum(partial_hidden.astype(jnp.bfloat16), 'col').astype(jnp.float32)]
    pallas_call x0 -> x1, Pallas kernels: none -> 135 us  [body(): pl.pallas_call(kernel, out_shape=(jax.ShapeDtypeStruct((CAP, width), BF),...]
    dot_general x14 -> x0, matrix products: 26.2 us -> none  [the longest x4 7.94 us: sparse_apply(): jnp.einsum(pattern, selected, blocks, preferred_element_type=jnp.float32)]
    psum x1 -> x0, blocking collectives: 19.1 us -> none  [body(): total_count = lax.psum(counts[0], 'dp').astype(jnp.float32)]
    gather x4 -> x0, local copies, waits for them, and re-layouts: 8.63 us -> none  [sparse_apply(): jnp.take(operand.reshape(row_count, -1, block_size), in_index, axis=1)]
    convert_element_type x4 -> x0, other arithmetic: 5.15 us -> none  [the longest x1 3.15 us: body(): hidden_grad = (act_grad * gelu_slope(hidden)).astype(jnp.bfloat16)]
  transfers between devices with their start and end apart: 4 -> 0, of which waited for: 4 -> 0; matrix products, arithmetic and copies ran while one was open for 2% -> 0% of each run, Pallas kernels for 0% -> 0%
where the time goes in v1:
time: 143 us
  Pallas kernels  135 us (94%)
  local copies, waits for them, and re-layouts  5.88 us (4%)
    pallas_call x1, Pallas kernels, body(): pl.pallas_call(kernel, out_shape=(jax.ShapeDtypeStruct((CAP, width), BF),...  135 us
    unnamed x18, local copies, waits for them, and re-layouts  5.88 us

profile of v1, /device:TPU:1, one launch (start us, length us, event | category | flops | bytes accessed | tf_op | source)
XLA Modules:
  0.0 143.2 jit_solution(13079931306126584903)
XLA Ops:
  1.3 0.0 copy-start.5
  1.3 0.0 copy-start.6
  1.3 0.6 copy-done.5
  1.9 0.0 copy-done.6
  2.0 0.0 copy-start.3
  2.0 0.0 copy-start.4
  2.0 0.6 copy-done.3
  2.6 0.0 copy-done.4
  2.6 0.1 select_reduce_fusion
  2.7 0.5 broadcast_subtract_fusion
  3.2 135.4 %shard_map.120 = (bf16[256,1024]{1,0:T(8,128)(2,1)}, bf16[256,1024]{1,0:T(8,128)(2,1)}, f32[2,128,128]{2,1,0:T(8,128)}, f32[2,128,128]{2,1,0:T(8,128)}) custom-call(s32[1]{0:T(128)S(6)} %copy.17.counts, s32[128]{0:T(128)} %get-tuple-element.15.inv_up, s32[128]{0:T(128)} %get-tuple-element.14.inv_down, s32[32]{0:T(128)} %bitcast.19, s32[32]{0:T(128)} %bitcast.18, ...), custom_call_target="tpu_custom_call" | custom-call | tf_op jit(solution)/shard_map/pallas_call | solution.py:396
  138.6 0.0 copy-start
  138.6 1.9 %copy.18 = bf16[256,1024]{1,0:T(8,128)(2,1)} copy(bf16[256,1024]{1,0:T(8,128)(2,1)} %get-tuple-element.20) | data formatting | bytes 1048576
  140.5 0.0 copy-done
  140.5 0.0 copy-start.2
  140.5 0.8 copy.19
  141.3 0.2 copy-done.2
  141.6 0.0 copy-start.1
  141.6 0.7 copy.20
  142.2 0.3 copy-done.1
  142.5 0.7 copy.21
  (3 shorter events, 0.0 us)
Async XLA Ops:
  1.3 0.7 copy-start.5
  1.3 0.7 copy-start.6
  2.0 0.7 copy-start.3
  2.0 0.7 copy-start.4
  138.6 1.9 %copy-start = (bf16[256,1024]{1,0:T(8,128)(2,1)S(1)}, bf16[256,1024]{1,0:T(8,128)(2,1)}, u32[]{:S(2)}) copy-start(bf16[256,1024]{1,0:T(8,128)(2,1)} %get-tuple-element.21) | copy-start | bytes 1572868
  140.5 1.0 copy-start.2
  141.6 1.0 copy-start.1

commit v2 on v1

--- a/solution.py
+++ b/solution.py
@@ -14,7 +14,7 @@
 STEPS = 8
 TD = 8
 NB = 32
-LAG = 4
+LATE, NEAR, FAR = 2, 7, 9
 CH = 2 * B + 16
 QR = 32
 
@@ -166,20 +166,21 @@
         gacc[...] += dot(hg, wup[k], NT)
 
     def line(it, carry):
-        @pl.when(it < STEPS)
-        def _():
-            sum_step(it, first)
-            sum_step(it, 1 - first)
-
-        @pl.when(it >= LAG)
-        def _():
-            share_step(it - LAG, 1 - first)
-            share_step(it - LAG, first)
-            use_step(it - LAG)
-
+        def during(lag, step):
+            pl.when((it >= lag) & (it < lag + STEPS))(lambda: step(it - lag))
+
+        during(0, lambda k: sum_step(k, first))
+        during(LATE, lambda k: sum_step(k, 1 - first))
+        during(NEAR, lambda k: share_step(k, 1 - first))
+
+        def last(k):
+            share_step(k, first)
+            use_step(k)
+
+        during(FAR, last)
         return carry
 
-    lax.fori_loop(0, STEPS + LAG, line, 0)
+    lax.fori_loop(0, STEPS + FAR, line, 0)
 
     mine = pl.multiple_of(core * B, B)
     other = pl.multiple_of((1 - core) * B, B)

time: 143 us -> 114 us (0.80); the launches traced: 143 us -> 113 us
  Pallas kernels: 135 us -> 105 us
    pallas_call x1, Pallas kernels: 135 us -> 105 us  [body(): pl.pallas_call(kernel, out_shape=(jax.ShapeDtypeStruct((CAP, width), BF),...]
where the time goes in v2:
time: 114 us; the launch traced here: 113 us
  Pallas kernels  105 us (92%)
  local copies, waits for them, and re-layouts  5.88 us (5%)
  between operations  1.32 us (1%)
    pallas_call x1, Pallas kernels, body(): pl.pallas_call(kernel, out_shape=(jax.ShapeDtypeStruct((CAP, width), BF),...  105 us
    unnamed x18, local copies, waits for them, and re-layouts  5.88 us

profile of v2, /device:TPU:1, one launch (start us, length us, event | category | flops | bytes accessed | tf_op | source)
XLA Modules:
  0.0 112.5 jit_solution(4533021445178295862)
XLA Ops:
  1.3 0.0 copy-start.5
  1.3 0.0 copy-start.6
  1.3 0.6 copy-done.5
  1.9 0.0 copy-done.6
  2.0 0.0 copy-start.3
  2.0 0.0 copy-start.4
  2.0 0.6 copy-done.3
  2.6 0.0 copy-done.4
  2.6 0.1 select_reduce_fusion
  2.7 0.5 broadcast_subtract_fusion
  3.2 104.7 %shard_map.120 = (bf16[256,1024]{1,0:T(8,128)(2,1)}, bf16[256,1024]{1,0:T(8,128)(2,1)}, f32[2,128,128]{2,1,0:T(8,128)}, f32[2,128,128]{2,1,0:T(8,128)}) custom-call(s32[1]{0:T(128)S(6)} %copy.17.counts, s32[128]{0:T(128)} %get-tuple-element.15.inv_up, s32[128]{0:T(128)} %get-tuple-element.14.inv_down, s32[32]{0:T(128)} %bitcast.19, s32[32]{0:T(128)} %bitcast.18, ...), custom_call_target="tpu_custom_call" | custom-call | tf_op jit(solution)/shard_map/pallas_call | solution.py:397
  107.9 0.0 copy-start
  107.9 1.9 %copy.18 = bf16[256,1024]{1,0:T(8,128)(2,1)} copy(bf16[256,1024]{1,0:T(8,128)(2,1)} %get-tuple-element.20) | data formatting | bytes 1048576
  109.9 0.0 copy-done
  109.9 0.0 copy-start.2
  109.9 0.8 copy.19
  110.7 0.2 copy-done.2
  110.9 0.0 copy-start.1
  110.9 0.7 copy.20
  111.6 0.3 copy-done.1
  111.9 0.7 copy.21
  (3 shorter events, 0.0 us)
Async XLA Ops:
  1.3 0.7 copy-start.5
  1.3 0.7 copy-start.6
  2.0 0.7 copy-start.3
  2.0 0.7 copy-start.4
  107.9 1.9 %copy-start = (bf16[256,1024]{1,0:T(8,128)(2,1)S(1)}, bf16[256,1024]{1,0:T(8,128)(2,1)}, u32[]{:S(2)}) copy-start(bf16[256,1024]{1,0:T(8,128)(2,1)} %get-tuple-element.21) | copy-start | bytes 1572868
  109.9 1.0 copy-start.2
  110.9 1.0 copy-start.1

commit v3 on v0

v3 whole, which is shorter than its diff:
```python
import jax
import jax.numpy as jnp
from jax import lax
from jax.experimental import pallas as pl
from jax.experimental.pallas import tpu as pltpu
from jax.sharding import PartitionSpec as P

MESH = pl.DeviceIdType.MESH
BF = jnp.bfloat16
F32 = jnp.float32
B = 128
CAP = 256
MB_TOK = 64
COLS = 8
STEPS = 16
TD = 8
NB = 32
LATE, NEAR, FAR = 4, 14, 18
CH = B + 16
QR = 32
HW = 512

NT = (((1,), (1,)), ((), ()))
NN = (((1,), (0,)), ((), ()))


def dot(a, b, dims=NN):
    return lax.dot_general(a, b, dims, preferred_element_type=F32)


def kernel(
    counts, up_rows, up_cols, down_rows, down_cols,
    tokens_in, cotangent_in, up_in, down_in,
    y_out, g_out, gu_out, gd_out,
    tokens, cotangent, up_blocks, down_blocks, inv_v, inv_s, gm, tok_t, gm_t, wup, wdn, part, rbuf, ah, acts, yacc, gacc,
    fs, fr, ys, yr, yo, gbuf, xr, zbuf, zr,
    in_s, inv_sem, rs_s, rs_r, ag_s, ag_r, f_s, f_r, y_s, y_r, ya_s, ya_r, sb_s, sb_r, x_s, x_r, z_s, z_r,
):
    loads = [
        pltpu.make_async_copy(src, dst, in_s.at[i])
        for i, (src, dst) in enumerate(
            ((tokens_in, tokens), (up_in, up_blocks), (cotangent_in, cotangent), (down_in, down_blocks))
        )
    ]
    for load in loads:
        load.start()

    c = lax.axis_index("col")
    row = lax.axis_index("row")
    dp = lax.axis_index("dp")
    core = row % 2
    yi = row // 2
    hi = dp // 4
    xi = dp % 4
    count = counts[0]

    sibling = {"row": row + 1 - 2 * core}
    y_right = {"row": (row + 2) % 8}
    y_left = {"row": (row + 6) % 8}
    x_right = {"dp": hi * 4 + (xi + 1) % 4}
    x_left = {"dp": hi * 4 + (xi + 3) % 4}
    z_right = {"dp": ((hi + 1) % 4) * 4 + xi}
    z_left = {"dp": ((hi + 3) % 4) * 4 + xi}

    def send(src, dst, s_sem, r_sem, device):
        return pltpu.make_async_remote_copy(
            src_ref=src, dst_ref=dst, send_sem=s_sem, recv_sem=r_sem,
            device_id=device, device_id_type=MESH,
        )

    barrier = pltpu.get_barrier_semaphore()
    for peer in (sibling, y_right, y_left, x_right, x_left, z_right, z_left):
        pl.semaphore_signal(barrier, inc=1, device_id=peer, device_id_type=MESH)

    @pl.when(c > 0)
    def _():
        pl.semaphore_signal(barrier, inc=1, device_id={"col": c - 1}, device_id_type=MESH)

    @pl.when(c < 3)
    def _():
        pl.semaphore_signal(barrier, inc=1, device_id={"col": c + 1}, device_id_type=MESH)

    lane = lax.broadcasted_iota(jnp.int32, (8, B), 1)
    for tile, (rows_in, cols_in, wide) in enumerate(((up_rows, up_cols, 16), (down_rows, down_cols, TD))):
        table = jnp.full((8, B), NB, jnp.int32)
        for k in range(NB):
            table = jnp.where(lane == rows_in[k] * wide + cols_in[k], k, table)
        inv_v[tile] = table
    tables = pltpu.make_async_copy(inv_v, inv_s, inv_sem)
    tables.start()

    live = (lax.broadcasted_iota(jnp.int32, (CAP, 1), 0) // MB_TOK < count).astype(F32)
    loads[2].wait()
    gm[...] = (cotangent[...].astype(F32) * live).astype(BF)
    loads[0].wait()
    loads[1].wait()
    loads[3].wait()
    tables.wait()

    inside = jnp.where((c > 0) & (c < 3), 1, 0)
    pl.semaphore_wait(barrier, 8 + inside)

    def place(s):
        q = c + s * (3 - 2 * c)
        return q, c + 1 - 2 * s, c - 1 + 2 * s

    def rs_copy(u, s, device):
        ref = rbuf.at[s * COLS + u % COLS, u // COLS]
        j = s * STEPS + u
        return send(ref, ref, rs_s.at[j], rs_r.at[j], {"col": device})

    def ag_copy(u, s, device):
        ref = ah.at[s * COLS + u % COLS, u // COLS]
        j = s * STEPS + u
        return send(ref, ref, ag_s.at[j], ag_r.at[j], {"col": device})

    def enter(k, kind, both):
        for s in range(2):
            part[k + COLS * s, kind] = both[:, s * B:(s + 1) * B]

        @pl.when(c == 0)
        def _():
            rbuf[k, kind] = both[:, :B].astype(BF)
            rs_copy(k + COLS * kind, 0, 1).start()

        @pl.when(c == 3)
        def _():
            rbuf[k + COLS, kind] = both[:, B:].astype(BF)
            rs_copy(k + COLS * kind, 1, 2).start()

    def hidden_partials(k, carry):
        for s in range(2):
            for i in range(TD):
                iu = inv_s[0, 0, i * 16 + k + COLS * s]
                blk = up_blocks[jnp.minimum(iu, NB - 1)]
                wup[k, i * B:(i + 1) * B, s * B:(s + 1) * B] = jnp.where(iu < NB, blk, jnp.zeros_like(blk))
        enter(k, 0, dot(tokens[...], wup[k]))
        return carry

    def act_partials(k, carry):
        for s in range(2):
            for i in range(TD):
                idn = inv_s[1, 0, (k + COLS * s) * TD + i]
                blk = down_blocks[jnp.minimum(idn, NB - 1)]
                wdn[k, s * B:(s + 1) * B, i * B:(i + 1) * B] = jnp.where(idn < NB, blk, jnp.zeros_like(blk))
        enter(k, 1, dot(gm[...], wdn[k], NT))
        return carry

    lax.fori_loop(0, COLS, hidden_partials, 0)
    lax.fori_loop(0, COLS, act_partials, 0)

    yacc[...] = jnp.zeros_like(yacc)
    gacc[...] = jnp.zeros_like(gacc)
    for i in range(TD):
        tok_t[i] = tokens[:, i * B:(i + 1) * B].T
        gm_t[i] = gm[:, i * B:(i + 1) * B].T

    first = c // 2

    def sum_step(u, s):
        q, nxt, prv = place(s)
        j = s * COLS + u % COLS
        kind = u // COLS

        @pl.when(q > 0)
        def _():
            rs_copy(u, s, nxt).wait_recv()

        @pl.when((q > 0) & (q < 3))
        def _():
            rbuf[j, kind] = (rbuf[j, kind].astype(F32) + part[j, kind]).astype(BF)
            rs_copy(u, s, nxt).start()

        @pl.when((q == 3) & (kind == 0))
        def _():
            h = rbuf[j, 0].astype(F32) + part[j, 0]
            cdf = 0.5 * (1.0 + lax.erf(h * 0.7071067811865476))
            ah[j, 0] = (h * cdf).astype(BF)
            ag_copy(u, s, prv).start()
            part[j, 0] = cdf + h * jnp.exp(-0.5 * h * h) * 0.3989422804014327

        @pl.when((q == 3) & (kind == 1))
        def _():
            a = rbuf[j, 1].astype(F32) + part[j, 1]
            ah[j, 1] = (a * part[j, 0]).astype(BF)
            ag_copy(u, s, prv).start()

    def share_step(u, s):
        q, nxt, prv = place(s)

        @pl.when(q < 3)
        def _():
            ag_copy(u, s, prv).wait_recv()

        @pl.when((q > 0) & (q < 3))
        def _():
            ag_copy(u, s, prv).start()

    def line(kind):
        def body(it, carry):
            def during(lag, step):
                pl.when((it >= lag) & (it < lag + STEPS))(lambda: step(it - lag))

            if kind == 0:
                during(0, lambda u: sum_step(u, first))
                during(LATE, lambda u: sum_step(u, 1 - first))
            during(NEAR, lambda u: share_step(u, 1 - first))

            def last(u):
                share_step(u, first)
                k = u % COLS
                one, two = ah[k, kind], ah[k + COLS, kind]
                both = jnp.concatenate([one, two], axis=1)
                if kind == 0:
                    acts[k] = one
                    acts[k + COLS] = two
                    yacc[...] += dot(both, wdn[k])
                else:
                    gacc[...] += dot(both, wup[k], NT)

            during(FAR, last)
            return carry

        return body

    count_rows = jnp.zeros((16, B), F32) + count.astype(F32)

    order = [(hi + 2) % 4, (hi + 1) % 4, (hi + 3) % 4, hi]
    x1, x2, x3 = (xi + 1) % 4, (xi + 2) % 4, (xi + 3) % 4
    y1, y2, y3 = (yi + 1) % 4, (yi + 2) % 4, (yi + 3) % 4

    def size(arr, b):
        return CH if arr == 1 and b == 0 else B

    def grads(arr, g):
        def body(xq, carry):
            for b in range(2):
                k = (order[g] * 4 + xq) * 2 + b
                if arr == 0:
                    block = dot(gm_t[down_cols[k]], acts[down_rows[k]])
                else:
                    block = dot(tok_t[up_rows[k]], ah[up_cols[k], 1])
                gbuf[arr, g, xq, b, :B, :] = block.astype(BF)
            if arr == 1:
                gbuf[arr, g, xq, 0, B:, :] = count_rows.astype(BF)
            return carry

        lax.fori_loop(0, 4, body, 0)

    def half_of(m):
        return (0, 1, 1, 0, 0, 1)[m]

    def x_msg(arr, g, m):
        b = half_of(m)
        rows = pl.ds(0, size(arr, b))
        place_of = (x2, x2, x1, x3)
        src = gbuf.at[arr, g, place_of[m], b, rows] if m < 4 else xr.at[arr, g, m - 4, rows]
        return send(
            src, xr.at[arr, g, m, rows], x_s.at[arr, g, m], x_r.at[arr, g, m], x_left if m % 2 else x_right
        )

    def x_start(arr, g):
        for m in range(4):
            x_msg(arr, g, m).start()

    def x_relay(arr, g):
        for m in range(2):
            n = size(arr, m)
            x_msg(arr, g, m).wait_recv()
            near = x3 if m else x1
            xr[arr, g, m, :n] = (xr[arr, g, m, :n].astype(F32) + gbuf[arr, g, near, m, :n].astype(F32)).astype(BF)
            x_msg(arr, g, m + 4).start()

    def x_final(arr, g):
        for m in range(2, 6):
            x_msg(arr, g, m).wait_recv()
        for b in range(2):
            n = size(arr, b)
            one, two = (2, 5) if b else (3, 4)
            full = gbuf[arr, g, xi, b, :n].astype(F32) + xr[arr, g, one, :n].astype(F32)
            zbuf[arr, g, b, :n] = (full + xr[arr, g, two, :n].astype(F32)).astype(BF)

    def z_msg(arr, m):
        b = half_of(m)
        rows = pl.ds(0, size(arr, b))
        src = zbuf.at[arr, (0, 0, 1, 2)[m], b, rows] if m < 4 else zr.at[arr, m - 4, rows]
        return send(src, zr.at[arr, m, rows], z_s.at[arr, m], z_r.at[arr, m], z_left if m % 2 else z_right)

    def z_relay(arr, m):
        n = size(arr, m)
        z_msg(arr, m).wait_recv()
        zr[arr, m, :n] = (zr[arr, m, :n].astype(F32) + zbuf[arr, 1 + m, m, :n].astype(F32)).astype(BF)
        z_msg(arr, m + 4).start()

    def z_final(arr, b):
        for m in (2, 5) if b else (3, 4):
            z_msg(arr, m).wait_recv()
        n = size(arr, b)
        one, two = (2, 5) if b else (3, 4)
        return zbuf[arr, 3, b, :n].astype(F32) + zr[arr, one, :n].astype(F32) + zr[arr, two, :n].astype(F32)

    accs = (yacc, gacc)
    mine = pl.multiple_of(core * B, B)
    other = pl.multiple_of((1 - core) * B, B)

    def pair(a):
        return send(fs.at[a], fr.at[a], f_s.at[a], f_r.at[a], sibling)

    def term(a, chunk, half):
        rows = pl.ds(pl.multiple_of(core * B + chunk * QR, QR), QR)
        return accs[a][rows, half * HW:(half + 1) * HW]

    def row_msg(a, m):
        src = ys.at[a, m] if m < 4 else yr.at[a, m - 4]
        return send(src, yr.at[a, m], y_s.at[a, m], y_r.at[a, m], y_left if m % 2 else y_right)

    def share_ref(a, chunk, m):
        return yo.at[core * 4 + chunk, a, half_of(m) if m in (2, 3) else m % 2]

    def share_msg(a, m):
        ref = share_ref(a, (yi, yi, yi, yi, y3, y1)[m], m)
        return send(ref, ref, ya_s.at[a, m], ya_r.at[a, m], y_left if m % 2 else y_right)

    def share_in(a, m):
        ref = share_ref(a, (y3, y1, y3, y1, y2, y2)[m], m)
        return send(ref, ref, ya_s.at[a, m], ya_r.at[a, m], y_left if m % 2 else y_right)

    def twin(a, m, half):
        ref = yo.at[half * 4 + (yi, y3, y1, y2)[m], a]
        return send(ref, ref, sb_s.at[a, m], sb_r.at[a, m], sibling)

    def row_pair(a):
        fs[a] = accs[a][pl.ds(other, B), :].astype(BF)
        pair(a).start()

    def row_start(a):
        pair(a).wait_recv()
        accs[a][pl.ds(mine, B), :] += fr[a].astype(F32)
        for m in range(4):
            ys[a, m] = term(a, (y2, y2, y1, y3)[m], half_of(m)).astype(BF)
            row_msg(a, m).start()

    def row_relay(a):
        for m in range(2):
            row_msg(a, m).wait_recv()
            yr[a, m] = (yr[a, m].astype(F32) + term(a, (y1, y3)[m], m)).astype(BF)
            row_msg(a, m + 4).start()

    def row_final(a):
        for m in range(2, 6):
            row_msg(a, m).wait_recv()
        for b in range(2):
            one, two = (2, 5) if b else (3, 4)
            full = term(a, yi, b) + yr[a, one].astype(F32) + yr[a, two].astype(F32)
            if a == 0:
                full = full * (core * 2 + yi // 2 < count).astype(F32)
            yo[core * 4 + yi, a, b] = full.astype(BF)
        for m in range(4):
            share_msg(a, m).start()
        twin(a, 0, core).start()

    def row_pass(a):
        for m in range(2):
            share_in(a, m).wait_recv()
            share_msg(a, m + 4).start()
        for m in range(2):
            share_in(a, m + 2).wait_recv()
            twin(a, m + 1, core).start()

    def row_end(a):
        share_in(a, 4).wait_recv()
        share_in(a, 5).wait_recv()
        twin(a, 3, core).start()

    def row_out(a, out):
        for m in range(4):
            twin(a, m, 1 - core).wait_recv()
        for chunk in range(8):
            for b in range(2):
                out[chunk * QR:(chunk + 1) * QR, b * HW:(b + 1) * HW] = yo[chunk, a, b]

    after = FAR + COLS
    lax.fori_loop(0, after, line(0), 0)

    def on(first_step, steps):
        lax.fori_loop(after + first_step, after + first_step + steps, line(1), 0)

    row_pair(0)
    grads(0, 0)
    x_start(0, 0)
    grads(0, 1)
    x_start(0, 1)
    on(0, 1)
    grads(0, 2)
    x_start(0, 2)
    grads(0, 3)
    x_start(0, 3)
    on(1, 1)
    row_start(0)
    x_relay(0, 0)
    on(2, 2)
    x_relay(0, 1)
    row_relay(0)
    on(4, 1)
    x_relay(0, 2)
    x_relay(0, 3)
    on(5, 1)
    row_final(0)
    x_final(0, 0)
    z_msg(0, 0).start()
    z_msg(0, 1).start()
    on(6, 2)

    row_pair(1)
    grads(1, 0)
    x_start(1, 0)
    x_final(0, 1)
    z_msg(0, 2).start()
    x_final(0, 2)
    z_msg(0, 3).start()
    grads(1, 1)
    x_start(1, 1)
    row_start(1)
    x_relay(1, 0)
    grads(1, 2)
    x_start(1, 2)
    z_relay(0, 0)
    z_relay(0, 1)
    x_relay(1, 1)
    row_relay(1)
    grads(1, 3)
    x_start(1, 3)
    x_final(1, 0)
    z_msg(1, 0).start()
    z_msg(1, 1).start()
    x_relay(1, 2)
    row_pass(0)
    row_final(1)
    x_final(1, 1)
    z_msg(1, 2).start()
    x_relay(1, 3)
    x_final(1, 2)
    z_msg(1, 3).start()
    row_end(0)
    row_pass(1)
    x_final(0, 3)
    x_final(1, 3)
    row_out(0, y_out)
    down0 = z_final(0, 0)
    down1 = z_final(0, 1)
    row_end(1)
    z_relay(1, 0)
    z_relay(1, 1)
    row_out(1, g_out)

    up0 = z_final(1, 0)
    total = up0[B:B + 1, :]
    gu_out[0] = up0[:B, :] / total
    gd_out[0] = (down0 / total).T
    gd_out[1] = (down1 / total).T
    gu_out[1] = z_final(1, 1) / total

    for s in range(2):
        q, nxt, prv = place(s)

        @pl.when(q < 3)
        def _(s=s, nxt=nxt):
            lax.fori_loop(0, STEPS, lambda u, v: (rs_copy(u, s, nxt).wait_send(), v)[1], 0)

        @pl.when(q > 0)
        def _(s=s, prv=prv):
            lax.fori_loop(0, STEPS, lambda u, v: (ag_copy(u, s, prv).wait_send(), v)[1], 0)

    for arr in range(2):
        pair(arr).wait_send()
        for m in range(6):
            row_msg(arr, m).wait_send()
            share_msg(arr, m).wait_send()
            z_msg(arr, m).wait_send()
            for g in range(4):
                x_msg(arr, g, m).wait_send()
        for m in range(4):
            twin(arr, m, core).wait_send()


def store(y, g, u, d, y_to, g_to, u_to, d_to, y_v, g_v, u_v, d_v, in_sem, out_sem):
    arrays = ((y, y_v, y_to), (g, g_v, g_to), (u, u_v, u_to), (d, d_v, d_to))
    into = [pltpu.make_async_copy(src, mid, in_sem.at[i]) for i, (src, mid, dst) in enumerate(arrays)]
    out = [pltpu.make_async_copy(mid, dst, out_sem.at[i]) for i, (src, mid, dst) in enumerate(arrays)]
    for copy in into:
        copy.start()
    for i in range(4):
        into[i].wait()
        out[i].start()
    for copy in out:
        copy.wait()


def body(tokens, cotangent, counts, up_blocks, up_rows, up_cols, down_blocks, down_rows, down_cols):
    ur, uc = up_rows[0, 0], up_cols[0, 0]
    dr, dc = down_rows[0, 0], down_cols[0, 0]
    smem = pl.BlockSpec(memory_space=pltpu.SMEM)
    vmem = pl.BlockSpec(memory_space=pltpu.VMEM)
    hbm = pl.BlockSpec(memory_space=pltpu.HBM)
    width = TD * B
    dma = pltpu.SemaphoreType.DMA
    shapes = (
        jax.ShapeDtypeStruct((CAP, width), BF),
        jax.ShapeDtypeStruct((CAP, width), BF),
        jax.ShapeDtypeStruct((2, B, B), F32),
        jax.ShapeDtypeStruct((2, B, B), F32),
    )
    results = pl.pallas_call(
        kernel,
        out_shape=shapes,
        in_specs=[smem] * 5 + [hbm] * 4,
        out_specs=(vmem,) * 4,
        scratch_shapes=[
            pltpu.VMEM((CAP, width), BF),
            pltpu.VMEM((CAP, width), BF),
            pltpu.VMEM((NB, B, B), BF),
            pltpu.VMEM((NB, B, B), BF),
            pltpu.VMEM((2, 8, B), jnp.int32),
            pltpu.SMEM((2, 8, B), jnp.int32),
            pltpu.VMEM((CAP, width), BF),
            pltpu.VMEM((TD, B, CAP), BF),
            pltpu.VMEM((TD, B, CAP), BF),
            pltpu.VMEM((STEPS, width, 2 * B), BF),
            pltpu.VMEM((STEPS, 2 * B, width), BF),
            pltpu.VMEM((16, 2, CAP, B), F32),
            pltpu.VMEM((16, 2, CAP, B), BF),
            pltpu.VMEM((16, 2, CAP, B), BF),
            pltpu.VMEM((16, CAP, B), BF),
            pltpu.VMEM((CAP, width), F32),
            pltpu.VMEM((CAP, width), F32),
            pltpu.VMEM((2, B, width), BF),
            pltpu.VMEM((2, B, width), BF),
            pltpu.VMEM((2, 4, QR, HW), BF),
            pltpu.VMEM((2, 6, QR, HW), BF),
            pltpu.VMEM((8, 2, 2, QR, HW), BF),
            pltpu.VMEM((2, 4, 4, 2, CH, B), BF),
            pltpu.VMEM((2, 4, 6, CH, B), BF),
            pltpu.VMEM((2, 4, 2, CH, B), BF),
            pltpu.VMEM((2, 6, CH, B), BF),
            dma((4,)), dma, dma((32,)), dma((32,)), dma((32,)), dma((32,)),
            dma((2,)), dma((2,)), dma((2, 6)), dma((2, 6)), dma((2, 6)), dma((2, 6)), dma((2, 4)), dma((2, 4)),
            dma((2, 4, 6)), dma((2, 4, 6)), dma((2, 6)), dma((2, 6)),
        ],
        compiler_params=pltpu.CompilerParams(
            collective_id=0, has_side_effects=True, vmem_limit_bytes=56 << 20
        ),
    )(counts, ur, uc, dr, dc, tokens, cotangent, up_blocks[0, 0], down_blocks[0, 0])
    y_out, g_out, gu, gd = pl.pallas_call(
        store,
        out_shape=shapes,
        in_specs=[hbm] * 4,
        out_specs=(hbm,) * 4,
        scratch_shapes=[pltpu.VMEM(shape.shape, shape.dtype) for shape in shapes] + [dma((4,)), dma((4,))],
    )(*results)
    return y_out, g_out, gu[None, None], gd[None, None]


def solution(mesh):
    return jax.shard_map(
        body,
        mesh=mesh,
        in_specs=(
            P("dp", "col"),
            P("dp", "col"),
            P("dp"),
            P("col", "row", None, None, None),
            P("col", "row", None),
            P("col", "row", None),
            P("row", "col", None, None, None),
            P("row", "col", None),
            P("row", "col", None),
        ),
        out_specs=(
            P("dp", "col"),
            P("dp", "col"),
            P("col", "row", "dp", None, None),
            P("row", "col", "dp", None, None),
        ),
        check_vma=False,
    )
```

time: 482 us -> 105 us (0.22)
  waiting for transfers between devices: 390 us -> 0 us
  Pallas kernels: 0 us -> 102 us
  matrix products: 26.2 us -> 0 us
  local copies, waits for them, and re-layouts: 19.7 us -> 0 us
  blocking collectives: 19.1 us -> 0 us
  between operations: 15.3 us -> 1.29 us
  other arithmetic: 11 us -> 0 us
    reduce_scatter x2 -> x0, waiting for transfers between devices: 228 us -> none  [the longest x1 117 us: body(): lax.psum_scatter(slab_terms(activation, grad_mask, down_from, down_into,...]
    psum x2 -> x0, waiting for transfers between devices: 162 us -> none  [the longest x1 114 us: body(): lax.psum(partial_hidden.astype(jnp.bfloat16), 'col').astype(jnp.float32)]
    pallas_call x0 -> x2, Pallas kernels: none -> 102 us  [the longest x1 100 us: body(): pl.pallas_call(kernel, out_shape=shapes, in_specs=[smem] * 5 + [hbm] * 4,...]
    dot_general x14 -> x0, matrix products: 26.2 us -> none  [the longest x4 7.94 us: sparse_apply(): jnp.einsum(pattern, selected, blocks, preferred_element_type=jnp.float32)]
    psum x1 -> x0, blocking collectives: 19.1 us -> none  [body(): total_count = lax.psum(counts[0], 'dp').astype(jnp.float32)]
    gather x4 -> x0, local copies, waits for them, and re-layouts: 8.63 us -> none  [sparse_apply(): jnp.take(operand.reshape(row_count, -1, block_size), in_index, axis=1)]
    convert_element_type x4 -> x0, other arithmetic: 5.15 us -> none  [the longest x1 3.15 us: body(): hidden_grad = (act_grad * gelu_slope(hidden)).astype(jnp.bfloat16)]
  transfers between devices with their start and end apart: 4 -> 0, of which waited for: 4 -> 0; matrix products, arithmetic and copies ran while one was open for 2% -> 0% of each run, Pallas kernels for 0% -> 0%
where the time goes in v3:
time: 105 us; the launch traced here: 104 us
  Pallas kernels  102 us (97%)
  between operations  1.29 us (1%)
    pallas_call x1, Pallas kernels, body(): pl.pallas_call(kernel, out_shape=shapes, in_specs=[smem] * 5 + [hbm] * 4,...  100 us
    pallas_call x1, Pallas kernels, body(): pl.pallas_call(store, out_shape=shapes, in_specs=[hbm] * 4, out_specs=(hb...  2.15 us

profile of v3, /device:TPU:1, one launch (start us, length us, event | category | flops | bytes accessed | tf_op | source)
XLA Modules:
  0.0 103.8 jit_solution(5531557764445852648)
XLA Ops:
  1.3 100.3 %shard_map.120 = (bf16[256,1024]{1,0:T(8,128)(2,1)}, bf16[256,1024]{1,0:T(8,128)(2,1)}, f32[2,128,128]{2,1,0:T(8,128)}, f32[2,128,128]{2,1,0:T(8,128)}) custom-call(s32[1]{0:T(128)S(6)} %copy.13.counts, s32[32]{0:T(128)} %bitcast.10, s32[32]{0:T(128)} %bitcast.11, s32[32]{0:T(128)} %bitcast.12, s32[32]{0:T(128)} %bitcast.13, bf16[256,1024]{1,0:T(8,128)(2,1)} %tokens_in.1, ...), custom_call_target="tpu_custom_call" | custom-call | tf_op jit(solution)/shard_map/pallas_call | solution.py:513
  101.6 2.2 %shard_map.121 = (bf16[256,1024]{1,0:T(8,128)(2,1)}, bf16[256,1024]{1,0:T(8,128)(2,1)}, f32[2,128,128]{2,1,0:T(8,128)}, f32[2,128,128]{2,1,0:T(8,128)}) custom-call(bf16[256,1024]{1,0:T(8,128)(2,1)} %get-tuple-element.12.y, bf16[256,1024]{1,0:T(8,128)(2,1)} %get-tuple-element.13.g, f32[2,128,128]{2,1,0:T(8,128)} %get-tuple-element.14.u, ...), custom_call_target="tpu_custom_call" | custom-call | tf_op jit(solution)/shard_map/pallas_call | solution.py:553

commit v4 on v3

--- a/solution.py
+++ b/solution.py
@@ -151,9 +151,10 @@
 
     yacc[...] = jnp.zeros_like(yacc)
     gacc[...] = jnp.zeros_like(gacc)
-    for i in range(TD):
-        tok_t[i] = tokens[:, i * B:(i + 1) * B].T
-        gm_t[i] = gm[:, i * B:(i + 1) * B].T
+    def transposes(i):
+        columns = pl.ds(pl.multiple_of(i * B, B), B)
+        tok_t[i] = tokens[:, columns].T
+        gm_t[i] = gm[:, columns].T
 
     first = c // 2
 
@@ -204,6 +205,7 @@
             if kind == 0:
                 during(0, lambda u: sum_step(u, first))
                 during(LATE, lambda u: sum_step(u, 1 - first))
+                pl.when((it >= COLS) & (it < 2 * COLS))(lambda: transposes(it - COLS))
             during(NEAR, lambda u: share_step(u, 1 - first))
 
             def last(u):
@@ -406,14 +408,14 @@
     x_relay(0, 3)
     on(5, 1)
     row_final(0)
+    on(6, 2)
+
+    row_pair(1)
+    grads(1, 0)
+    x_start(1, 0)
     x_final(0, 0)
     z_msg(0, 0).start()
     z_msg(0, 1).start()
-    on(6, 2)
-
-    row_pair(1)
-    grads(1, 0)
-    x_start(1, 0)
     x_final(0, 1)
     z_msg(0, 2).start()
     x_final(0, 2)
@@ -448,9 +450,9 @@
     row_out(0, y_out)
     down0 = z_final(0, 0)
     down1 = z_final(0, 1)
-    row_end(1)
     z_relay(1, 0)
     z_relay(1, 1)
+    row_end(1)
     row_out(1, g_out)
 
     up0 = z_final(1, 0)

time: 105 us -> 102 us (0.971)
  Pallas kernels: 102 us -> 100 us
    pallas_call x1, Pallas kernels: 100 us -> 98.3 us  [body(): pl.pallas_call(kernel, out_shape=shapes, in_specs=[smem] * 5 + [hbm] * 4,...]
where the time goes in v4:
time: 102 us
  Pallas kernels  100 us (98%)
  between operations  1.29 us (1%)
    pallas_call x1, Pallas kernels, body(): pl.pallas_call(kernel, out_shape=shapes, in_specs=[smem] * 5 + [hbm] * 4,...  98.3 us
    pallas_call x1, Pallas kernels, body(): pl.pallas_call(store, out_shape=shapes, in_specs=[hbm] * 4, out_specs=(hb...  2.15 us

profile of v4, /device:TPU:1, one launch (start us, length us, event | category | flops | bytes accessed | tf_op | source)
XLA Modules:
  0.0 101.8 jit_solution(16313728256982267204)
XLA Ops:
  1.3 98.3 %shard_map.120 = (bf16[256,1024]{1,0:T(8,128)(2,1)}, bf16[256,1024]{1,0:T(8,128)(2,1)}, f32[2,128,128]{2,1,0:T(8,128)}, f32[2,128,128]{2,1,0:T(8,128)}) custom-call(s32[1]{0:T(128)S(6)} %copy.13.counts, s32[32]{0:T(128)} %bitcast.10, s32[32]{0:T(128)} %bitcast.11, s32[32]{0:T(128)} %bitcast.12, s32[32]{0:T(128)} %bitcast.13, bf16[256,1024]{1,0:T(8,128)(2,1)} %tokens_in.1, ...), custom_call_target="tpu_custom_call" | custom-call | tf_op jit(solution)/shard_map/pallas_call | solution.py:515
  99.6 2.2 %shard_map.121 = (bf16[256,1024]{1,0:T(8,128)(2,1)}, bf16[256,1024]{1,0:T(8,128)(2,1)}, f32[2,128,128]{2,1,0:T(8,128)}, f32[2,128,128]{2,1,0:T(8,128)}) custom-call(bf16[256,1024]{1,0:T(8,128)(2,1)} %get-tuple-element.12.y, bf16[256,1024]{1,0:T(8,128)(2,1)} %get-tuple-element.13.g, f32[2,128,128]{2,1,0:T(8,128)} %get-tuple-element.14.u, ...), custom_call_target="tpu_custom_call" | custom-call | tf_op jit(solution)/shard_map/pallas_call | solution.py:555

commit v5 on v4

--- a/solution.py
+++ b/solution.py
@@ -89,12 +89,8 @@
     tables = pltpu.make_async_copy(inv_v, inv_s, inv_sem)
     tables.start()
 
-    live = (lax.broadcasted_iota(jnp.int32, (CAP, 1), 0) // MB_TOK < count).astype(F32)
-    loads[2].wait()
-    gm[...] = (cotangent[...].astype(F32) * live).astype(BF)
     loads[0].wait()
     loads[1].wait()
-    loads[3].wait()
     tables.wait()
 
     inside = jnp.where((c > 0) & (c < 3), 1, 0)
@@ -147,6 +143,10 @@
         return carry
 
     lax.fori_loop(0, COLS, hidden_partials, 0)
+    live = (lax.broadcasted_iota(jnp.int32, (CAP, 1), 0) // MB_TOK < count).astype(F32)
+    loads[2].wait()
+    gm[...] = (cotangent[...].astype(F32) * live).astype(BF)
+    loads[3].wait()
     lax.fori_loop(0, COLS, act_partials, 0)
 
     yacc[...] = jnp.zeros_like(yacc)

time: 102 us -> 102 us (level)
  no operation moved by 1% of the time
where the time goes in v5:
time: 102 us
  Pallas kernels  101 us (99%)
  between operations  1.29 us (1%)
    pallas_call x1, Pallas kernels, body(): pl.pallas_call(kernel, out_shape=shapes, in_specs=[smem] * 5 + [hbm] * 4,...  98.5 us
    pallas_call x1, Pallas kernels, body(): pl.pallas_call(store, out_shape=shapes, in_specs=[hbm] * 4, out_specs=(hb...  2.15 us

profile of v5, /device:TPU:1, one launch (start us, length us, event | category | flops | bytes accessed | tf_op | source)
XLA Modules:
  0.0 101.9 jit_solution(17716678633550976854)
XLA Ops:
  1.3 98.5 %shard_map.120 = (bf16[256,1024]{1,0:T(8,128)(2,1)}, bf16[256,1024]{1,0:T(8,128)(2,1)}, f32[2,128,128]{2,1,0:T(8,128)}, f32[2,128,128]{2,1,0:T(8,128)}) custom-call(s32[1]{0:T(128)S(6)} %copy.13.counts, s32[32]{0:T(128)} %bitcast.10, s32[32]{0:T(128)} %bitcast.11, s32[32]{0:T(128)} %bitcast.12, s32[32]{0:T(128)} %bitcast.13, bf16[256,1024]{1,0:T(8,128)(2,1)} %tokens_in.1, ...), custom_call_target="tpu_custom_call" | custom-call | tf_op jit(solution)/shard_map/pallas_call | solution.py:515
  99.8 2.2 %shard_map.121 = (bf16[256,1024]{1,0:T(8,128)(2,1)}, bf16[256,1024]{1,0:T(8,128)(2,1)}, f32[2,128,128]{2,1,0:T(8,128)}, f32[2,128,128]{2,1,0:T(8,128)}) custom-call(bf16[256,1024]{1,0:T(8,128)(2,1)} %get-tuple-element.12.y, bf16[256,1024]{1,0:T(8,128)(2,1)} %get-tuple-element.13.g, f32[2,128,128]{2,1,0:T(8,128)} %get-tuple-element.14.u, ...), custom_call_target="tpu_custom_call" | custom-call | tf_op jit(solution)/shard_map/pallas_call | solution.py:555
